TPU v7x, 512 devices: a whole 4x8x8 slice. The times are simulated.
512 devices in a mesh: pert: 16 (over x_lo, y), doc: 32 (over x_hi, z, core).
Axes of the slice: x: 4 (x_hi: 2, x_lo: 2; x = x_hi * 2 + x_lo), y: 8, z: 8, core: 2. Of those that a mesh axis runs over, the one named last changes fastest.
Arguments:
- counts: int32 [16, 256, 16384], P('pert', 'doc'), may hold values from 1 to 11
- tile_mask: int32 [16, 256, 128], P('pert', 'doc'), may hold values 0 or 1
- member_topics: float32 [16, 256, 64], P('pert', 'doc'), may hold values from 0.05 to 0.5
- start_dict: float32 [16, 16384, 64], P('pert', 'doc'), may hold values from 0.05 to 0.5
- align_perm: int32 [16, 64], P('pert'), may hold values from 0 to 63, each once within a row
- base_counts: int32 [2048, 16384], P(('pert', 'doc')), may hold values from 1 to 11
- base_topics: float32 [2048, 64], P(('pert', 'doc')), may hold values from 0.05 to 0.5
Outputs:
- median_dict: float32 [32, 16, 32, 64], P('doc', 'pert')
- refit_topics: float32 [2048, 64], P(('pert', 'doc'))
Inputs may be any that keep to these rules, and one draw needn't show every extreme that they name: `align_perm`: each row is a permutation of 0 to 63.
All inputs are finite; a program needn't handle non-finite values. No bound on the sum of `tile_mask` on one device may be relied on, other than what follows from the above.
Results may differ from a plain program's by a relative error of at most 0.0003.
Values sent between devices are 32-bit elements; how exact they have to be, the bound alone decides.
A program may use at most 64 MiB of HBM per device.

v0:
```python
import jax
import jax.numpy as jnp
from jax import lax
from jax.sharding import PartitionSpec as P

UPDATES = 3
REFITS = 2


HIGHEST_PRECISION = lax.Precision.HIGHEST


def recon_wide(topics, dict_wide):
    return jnp.dot(topics, dict_wide, precision=HIGHEST_PRECISION)


def weight_update(topics, quotient, dict_wide, col_total):
    product = lax.dot_general(
        quotient, dict_wide, (((1,), (1,)), ((), ())), precision=HIGHEST_PRECISION
    )
    return topics * product / col_total


def middle(stacked):
    ordered = jnp.sort(stacked, axis=0)
    middle_at = stacked.shape[0] // 2
    return 0.5 * (ordered[middle_at - 1] + ordered[middle_at])


def occupied_counts(counts, mask, first_doc):
    doc_count, word_count = counts.shape
    tile_count = mask.shape[1]
    tile_width = word_count // tile_count
    tile_ids = lax.broadcasted_iota(jnp.int32, (doc_count, tile_count), 1)
    doc_ids = first_doc + lax.broadcasted_iota(jnp.int32, (doc_count, tile_count), 0)
    occupied = jnp.maximum(mask, (tile_ids == doc_ids % tile_count).astype(jnp.int32)).astype(
        jnp.float32
    )
    spread = (
        counts.astype(jnp.float32).reshape(doc_count, tile_count, tile_width) * occupied[:, :, None]
    )
    return spread.reshape(doc_count, word_count)


def per_device(counts, tile_mask, member_topics, start_dict, align_perm, base_counts, base_topics):
    doc_rows = counts.shape[1]
    weighted = occupied_counts(counts[0], tile_mask[0], lax.axis_index("doc") * doc_rows)
    full_dict = lax.all_gather(start_dict[0], "doc", axis=0, tiled=True)
    dict_wide = full_dict.T
    col_total = jnp.sum(dict_wide, axis=1)
    topics = member_topics[0]
    for iteration in range(UPDATES):
        quotient = weighted / recon_wide(topics, dict_wide)
        topics = weight_update(topics, quotient, dict_wide, col_total)
    quotient = weighted / recon_wide(topics, dict_wide)
    topic_load = lax.psum(jnp.sum(topics, axis=0), "doc")
    owned_rows = start_dict.shape[1]
    numerator = lax.psum_scatter(
        lax.dot_general(quotient, topics, (((0,), (0,)), ((), ())), precision=HIGHEST_PRECISION),
        "doc",
        scatter_dimension=0,
        tiled=True,
    )
    new_dict = start_dict[0] * numerator / topic_load
    topic_count = new_dict.shape[1]
    onehot = (
        lax.broadcasted_iota(jnp.int32, (topic_count, topic_count), 0) == align_perm[0][None, :]
    ).astype(jnp.float32)
    aligned = jnp.dot(new_dict, onehot, precision=HIGHEST_PRECISION)
    members = lax.axis_size("pert")
    sub_rows = owned_rows // members
    regrouped = lax.all_to_all(
        aligned.reshape(members, sub_rows, topic_count),
        "pert",
        split_axis=0,
        concat_axis=0,
        tiled=True,
    )
    median_rows = middle(regrouped)
    joined = lax.all_gather(median_rows, ("pert", "doc"), axis=0, tiled=True)
    reordered = joined.reshape(members, lax.axis_size("doc"), sub_rows, topic_count).transpose(
        1, 0, 2, 3
    )
    full_median = reordered.reshape(-1, topic_count)
    median_wide = full_median.T
    median_total = jnp.sum(median_wide, axis=1)
    base_weighted = base_counts.astype(jnp.float32)
    refit_weights = base_topics
    for iteration in range(REFITS):
        quotient_base = base_weighted / recon_wide(refit_weights, median_wide)
        refit_weights = weight_update(refit_weights, quotient_base, median_wide, median_total)
    return (median_rows[None, None], refit_weights)


def solution(mesh):
    return jax.shard_map(
        per_device,
        mesh=mesh,
        in_specs=(
            P("pert", "doc", None),
            P("pert", "doc", None),
            P("pert", "doc", None),
            P("pert", "doc", None),
            P("pert", None),
            P(("pert", "doc"), None),
            P(("pert", "doc"), None),
        ),
        out_specs=(P("doc", "pert", None, None), P(("pert", "doc"), None)),
        check_vma=False,
    )
```

profile of v0, /device:TPU:1, one launch (start us, length us, event | category | flops | bytes accessed | tf_op | source)
XLA Modules:
  0.0 1189.6 jit_solution(5882168527588189696)
XLA Ops:
  7.2 0.7 all-gather.5.cloned.1.call-update
  8.0 0.8 fusion.37
  8.8 0.1 copy.21
  8.9 101.3 %all-gather.5.cloned.1.call-done = f32[1,16384,64]{1,2,0:T(8,128)} async-done(((f32[1,512,64]{1,2,0:T(8,128)}), f32[1,16384,64]{1,2,0:T(8,128)}) %all-gather.5.cloned.1.call-update) | async-done | bytes 4194320 | tf_op jit(solution)/shard_map/all_gather | solution.py:48
  110.2 2.5 reduce_sum.27
  112.7 4.0 convolution_divide_fusion.3
  116.7 3.3 fusion.14
  120.0 2.1 convolution_divide_fusion.2
  122.1 3.3 fusion.20
  125.5 2.1 convolution_divide_fusion.1
  127.6 3.7 fusion.39
  131.3 2.1 convolution_divide_fusion
  133.4 5.0 fusion.40
  138.5 64.8 %psum.7 = f32[64]{0:T(128)S(1)} all-reduce(f32[64]{0:T(128)S(1)} %get-tuple-element.11), channel_id=1, replica_groups=mesh['pert'=16,'doc'=32] {'doc'}, use_global_device_ids=true, to_apply=%region_3.4 | all-reduce | flops 64 | bytes 512 | tf_op jit(solution)/shard_map/psum | solution.py:56
  203.4 63.1 %reduce-scatter.2.cloned.1.call-done = f32[512,64]{0,1:T(8,128)} async-done(((f32[16384,64]{0,1:T(8,128)}), f32[512,64]{0,1:T(8,128)}) %reduce-scatter.2.cloned.1.call-update) | async-done | bytes 131088 | tf_op jit(solution)/shard_map/reduce_scatter | solution.py:58
  266.5 1.4 fusion.32
  267.9 0.2 reshape.95
  268.1 13.8 %all_to_all.5 = f32[16,1,2048]{2,1,0:T(1,128)S(1)} all-to-all(f32[16,1,2048]{2,1,0:T(1,128)S(1)} %reshape.95), channel_id=1, replica_groups=mesh['pert'=16,'doc'=32] {'pert'}, dimensions={0} | all-to-all | bytes 262144 | tf_op jit(solution)/shard_map/all_to_all | solution.py:72
  281.9 0.5 broadcast.72
  282.4 0.9 reduce.7
  283.5 0.3 copy.23
  283.8 23.5 %sort.15 = (f32[16,32,64]{1,0,2:T(8,128)S(1)}, s32[16,32,64]{1,0,2:T(8,128)}) sort(f32[16,32,64]{1,0,2:T(8,128)S(1)} %copy.23, s32[16,32,64]{1,0,2:T(8,128)S(1)} %iota.31), dimensions={0}, to_apply=%region_4.5 | sort | flops 491520 | bytes 524288 | tf_op jit(solution)/shard_map/jit(sort)/sort | solution.py:25
  307.4 0.7 copy.24
  308.1 0.7 copy.26
  308.8 821.1 %all-gather.7.cloned.1.call-done = f32[1,16384,64]{2,0,1:T(1,128)} async-done(((f32[1,32,64]{2,0,1:T(1,128)}), f32[1,16384,64]{2,0,1:T(1,128)}) %all-gather.7.cloned.1.call-update) | async-done | bytes 4194320 | tf_op jit(solution)/shard_map/all_gather | solution.py:80
  1129.8 4.4 copy.25
  1134.3 3.2 copy-done.1
  1137.5 7.4 fusion
  1144.9 18.5 %reduce_sum.29 = f32[64]{0:T(128)S(1)} reduce(f32[1,16384,64]{2,0,1:T(1,128)} %all-gather.7.cloned.1.call-done, f32[]{:T(128)} %constant.36.clone.1), dimensions={0,1}, to_apply=%region_5.6 | reduce | flops 1048512 | bytes 4194564 | tf_op jit(solution)/shard_map/reduce_sum | solution.py:86
  1163.4 7.6 fusion.30
  1171.0 7.1 convolution_divide_fusion.4
  1178.1 4.7 fusion.29
  (27 shorter events, 0.4 us)
Async XLA Ops:
  7.2 105.5 %copy-start.3 = (s32[1,8,16384]{2,1,0:T(8,128)S(1)}, s32[1,8,16384]{2,1,0:T(8,128)}, u32[]{:S(2)}) copy-start(s32[1,8,16384]{2,1,0:T(8,128)} %param.7) | copy-start | bytes 1572868
  7.2 105.5 %copy-start.6 = (f32[1,8,64]{2,1,0:T(8,128)S(1)}, f32[1,8,64]{2,1,0:T(8,128)}, u32[]{:S(2)}) copy-start(f32[1,8,64]{2,1,0:T(8,128)} %param.9) | copy-start | bytes 6148
  7.2 103.0 %all-gather.5.cloned.1.call-start = ((), (), s32[]{:S(2)}) async-start(), calls=%async_computation.3 | async-start | bytes 4325376 | tf_op jit(solution)/shard_map/all_gather | solution.py:48
  7.9 258.6 %reduce-scatter.2.cloned.1.call-start = ((), (), s32[]{:S(2)}) async-start(), calls=%async_computation.2 | async-start | bytes 4325376 | tf_op jit(solution)/shard_map/reduce_scatter | solution.py:58
  112.7 4.0 copy-start
  133.4 133.1 %copy-start.5 = (f32[1,512,64]{1,2,0:T(8,128)S(1)}, f32[1,512,64]{1,2,0:T(8,128)}, u32[]{:S(2)}) copy-start(f32[1,512,64]{1,2,0:T(8,128)} %param.10) | copy-start | bytes 393220
  133.4 133.1 %copy-start.8 = (s32[1,64]{1,0:T(1,128)S(1)}, s32[1,64]{1,0:T(1,128)}, u32[]{:S(2)}) copy-start(s32[1,64]{1,0:T(1,128)} %param.11) | copy-start | bytes 772
  138.5 991.3 %all-gather.7.cloned.1.call-start = ((), (), s32[]{:S(2)}) async-start(), calls=%async_computation.4 | async-start | bytes 8404992 | tf_op jit(solution)/shard_map/all_gather | solution.py:80
  1129.8 7.7 copy-start.4
  1129.8 7.7 copy-start.7
  1134.3 3.2 copy-start.1
  1163.4 7.6 copy-start.2
Sparse Core Ops, SparseCore 0:
  11.4 98.7 all-gather.4
  138.6 127.8 reduce-scatter.1
  308.2 821.5 all-gather.6
where the time goes:
time: 1210 us; the launch traced here: 1190 us
  waiting for transfers between devices  986 us (81%)
  blocking collectives  78.6 us (6%)
  matrix products  53.9 us (4%)
  other arithmetic  46.3 us (4%)
  between operations  14.1 us (1%)
    all_gather x1, waiting for transfers between devices, per_device(): joined = lax.all_gather(median_rows, ('pert', 'doc'), axis=0, tiled=True)  821 us
    all_gather x1, waiting for transfers between devices, per_device(): full_dict = lax.all_gather(start_dict[0], 'doc', axis=0, tiled=True)  101 us
    psum x1, blocking collectives, per_device(): topic_load = lax.psum(jnp.sum(topics, axis=0), 'doc')  64.8 us
    reduce_scatter x1, waiting for transfers between devices, per_device(): lax.psum_scatter(lax.dot_general(quotient, topics, (((0,), (0,)), ((), ()...  63.1 us
    dot_general x6, matrix products, recon_wide(): return jnp.dot(topics, dict_wide, precision=HIGHEST_PRECISION)  24.8 us
  transfers between devices with their start and end apart: 3, of which 3 were waited for; matrix products, arithmetic and copies ran while one was open for 0% of the time, Pallas kernels for 0%

commit v1 on v0

v1 whole, which is shorter than its diff:
```python
import functools

import jax
import jax.numpy as jnp
from jax import lax
from jax.experimental import pallas as pl
from jax.experimental.pallas import tpu as pltpu
from jax.sharding import PartitionSpec as P

UPDATES = 3
REFITS = 2
NX = 2
NC = 2
NW = NX * NC
MESH = pl.DeviceIdType.MESH
F32 = jnp.float32
BF16 = jnp.bfloat16


def sort_pairs(count):
    pairs = []
    span = 1
    while span < count:
        step = span
        while step >= 1:
            for start in range(step % span, count - step, 2 * step):
                for at in range(min(step, count - start - step)):
                    low, high = start + at, start + at + step
                    if low // (2 * span) == high // (2 * span):
                        pairs.append((low, high))
            step //= 2
        span *= 2
    return pairs


def middle(rows):
    rows = list(rows)
    for low, high in sort_pairs(len(rows)):
        rows[low], rows[high] = jnp.minimum(rows[low], rows[high]), jnp.maximum(rows[low], rows[high])
    at = len(rows) // 2
    return 0.5 * (rows[at - 1] + rows[at])


def split2(x):
    high = x.astype(BF16)
    return high, (x - high.astype(F32)).astype(BF16)


def split3(x):
    high = x.astype(BF16)
    rest = x - high.astype(F32)
    mid = rest.astype(BF16)
    return high, mid, (rest - mid.astype(F32)).astype(BF16)


def pack(x):
    half = x.shape[0] // 2
    return jnp.concatenate([x[:half], x[half:]], axis=1)


def unpack(x):
    half = x.shape[1] // 2
    return jnp.concatenate([x[:, :half], x[:, half:]], axis=0)


def turn_tall(x):
    wide = jnp.concatenate([x, jnp.zeros_like(x)], axis=1)
    return wide.T[: x.shape[1]]


def turn_flat(x):
    tall = jnp.concatenate([x, jnp.zeros_like(x)], axis=0)
    return tall.T[:, : x.shape[0]]


def dot(a, b):
    return jnp.dot(a, b, preferred_element_type=F32)


def dot_nt(a, b):
    return lax.dot_general(a, b, (((1,), (1,)), ((), ())), preferred_element_type=F32)


def kernel(
    counts_ref, mask_ref, mtop_ref, dict_ref, perm_ref, base_ref, btop_ref,
    med_ref, refit_ref,
    masked, data4, data32, bsend, base4, mtop4, btop4, dgather, mgather, dsplit, msplit,
    mpartial, bpartial, topics_z, q3, p2_send, p2_recv, p3_recv,
    w_send, w_recv, b_send, b_recv, t_send, t_recv, u_send, u_recv, rd_send, rd_recv, rm_send, rm_recv,
    a_send, a_recv, z_send, z_recv, g_send, g_recv, s_send, s_recv, m_send, m_recv,
    *, np_, nz,
):
    wb, k = dict_ref.shape
    docs, bdocs = mtop_ref.shape[0], btop_ref.shape[0]
    p = lax.axis_index("pert")
    b = lax.axis_index("doc")
    xh, z, c = b // (nz * NC), (b // NC) % nz, b % NC
    w = xh * NC + c
    chunk = k // 2
    slab = wb // np_

    def w_device(at):
        return (p, (at // NC) * (nz * NC) + z * NC + at % NC)

    def z_device(at):
        return (p, xh * (nz * NC) + at * NC + c)

    def p_device(at):
        return (at, b)

    w_peers = [lax.rem(w + i, NW) for i in range(1, NW)]
    z_peers = [lax.rem(z + i, nz) for i in range(1, nz)]
    p_peers = [lax.rem(p + i, np_) for i in range(1, np_)]

    barrier = pltpu.get_barrier_semaphore()
    for peer in w_peers:
        pl.semaphore_signal(barrier, inc=1, device_id=w_device(peer), device_id_type=MESH)
    for peer in z_peers:
        pl.semaphore_signal(barrier, inc=1, device_id=z_device(peer), device_id_type=MESH)
    for peer in p_peers:
        pl.semaphore_signal(barrier, inc=1, device_id=p_device(peer), device_id_type=MESH)

    tiles = mask_ref.shape[1]
    tile_width = counts_ref.shape[1] // tiles
    per_block = wb // tile_width
    tile_ids = lax.broadcasted_iota(jnp.int32, (docs, tiles), 1)
    doc_ids = b * docs + lax.broadcasted_iota(jnp.int32, (docs, tiles), 0)
    occupied = jnp.maximum(mask_ref[...], (tile_ids == doc_ids % tiles).astype(jnp.int32)).astype(F32)

    for owner in range(NW):

        def mask_block(zb, carry, owner=owner):
            block = ((owner // NC) * nz + zb) * NC + owner % NC
            for j in range(per_block):
                tile = block * per_block + j
                seen = jnp.sum(jnp.where(tile_ids == tile, occupied, 0.0), axis=1, keepdims=True)
                at = pl.multiple_of(tile * tile_width, tile_width)
                masked[owner, zb, :, j * tile_width : (j + 1) * tile_width] = (
                    counts_ref[:, pl.ds(at, tile_width)].astype(F32) * seen
                )
            at = pl.multiple_of(block * wb, wb)
            bsend[owner, zb] = base_ref[:, pl.ds(at, wb)].astype(F32)
            return carry

        lax.fori_loop(0, nz, mask_block, 0)
    dgather[z] = turn_tall(dict_ref[...])

    pl.semaphore_wait(barrier, NW - 1 + nz - 1 + np_ - 1)

    sends = []

    def remote(src, dst, ssem, rsem, device):
        return pltpu.make_async_remote_copy(
            src_ref=src, dst_ref=dst, send_sem=ssem, recv_sem=rsem, device_id=device, device_id_type=MESH
        )

    def start(copy):
        copy.start()
        sends.append(copy)

    right, left = lax.rem(z + 1, nz), lax.rem(z + nz - 1, nz)
    last = nz // 2

    def ring_block(way, s):
        return lax.rem(z + nz - s, nz) if way == 0 else lax.rem(z + s, nz)

    def ring_chunks(way, s):
        return (0, 1) if s < last else (way,)

    def ring_copy(buf, ssem, rsem, way, s, ch):
        at = buf.at[ring_block(way, s), pl.ds(ch * chunk, chunk), :]
        return remote(at, at, ssem.at[way, s, ch], rsem.at[way, s, ch], z_device(right if way == 0 else left))

    def ring_first(buf, ssem, rsem):
        for ch in (0, 1):
            for way in (0, 1):
                if ch in ring_chunks(way, 1):
                    start(ring_copy(buf, ssem, rsem, way, 0, ch))

    def ring_step(buf, ssem, rsem, s):
        for ch in (0, 1):
            for way in (0, 1):
                if ch in ring_chunks(way, s):
                    here = buf.at[ring_block(way, s), pl.ds(ch * chunk, chunk), :]
                    remote(
                        here, here, ssem.at[way, s - 1, ch], rsem.at[way, s - 1, ch],
                        z_device(right if way == 0 else left),
                    ).wait_recv()
                    if s < last and ch in ring_chunks(way, s + 1):
                        start(ring_copy(buf, ssem, rsem, way, s, ch))

    def blocks_at(s):
        if s == 0 or s == last:
            return [ring_block(0, s)]
        return [ring_block(0, s), ring_block(1, s)]

    def split_block(buf, out, at):
        high, low = split2(buf[at])
        out[at, 0:k] = high
        out[at, k : 2 * k] = low
        out[at, 2 * k : 3 * k] = high

    def stack_topics(topics):
        high, low = split2(topics)
        return jnp.concatenate([high, high, low], axis=1)

    def rows_of(buf, at):
        return jnp.concatenate([buf[owner, at] for owner in range(NW)], axis=0)

    def block_term(stacked, buf, split, at):
        data = rows_of(buf, at)
        rows = data.shape[0]
        high, low = split2(data / dot(stacked, split[at]))
        both = dot_nt(jnp.concatenate([high, low], axis=0), split[at, 0 : 2 * k])
        return both[:rows] + both[rows:]

    def column_term(split, at):
        return dot_nt(jnp.ones((16, wb), BF16), split[at, 0 : 2 * k])[:8]

    def fold(x):
        return x[:, :k] + x[:, k:]

    def all_terms(stacked, buf, split):
        def one(at, acc):
            return acc + block_term(stacked, buf, split, at)

        return lax.fori_loop(0, nz, one, jnp.zeros((stacked.shape[0], 2 * k), F32))

    def exchange(partial, at, number, acc, columns):
        rows = acc.shape[0] // 2
        partial[at, w, 0:rows] = pack(fold(acc))
        sent = rows
        if columns is not None:
            partial[at, w, rows : rows + 8] = columns
            sent = rows + 8
        for i, peer in enumerate(w_peers):
            mine = partial.at[at, w, 0:sent]
            start(remote(mine, mine, a_send.at[number, i], a_recv.at[number, w], w_device(peer)))
        for i, peer in enumerate(w_peers):
            theirs = partial.at[at, peer, 0:sent]
            remote(theirs, theirs, a_send.at[number, i], a_recv.at[number, peer], w_device(peer)).wait_recv()
        total = partial[at, 0, 0:sent]
        for owner in range(1, NW):
            total = total + partial[at, owner, 0:sent]
        product = unpack(total[:rows])
        return product, (fold(total[rows : rows + 1]) if columns is not None else None)

    ring_first(dgather, rd_send, rd_recv)
    for i, peer in enumerate(w_peers):
        start(remote(mtop_ref, mtop4.at[w], t_send.at[i], t_recv.at[w], w_device(peer)))
        start(remote(btop_ref, btop4.at[w], u_send.at[i], u_recv.at[w], w_device(peer)))
        start(remote(masked.at[peer], data4.at[w], w_send.at[i], w_recv.at[w], w_device(peer)))
    data4[w] = masked[w]
    base4[w] = bsend[w]
    mtop4[w] = mtop_ref[...]
    btop4[w] = btop_ref[...]
    split_block(dgather, dsplit, z)

    columns = column_term(dsplit, z)
    for s in range(1, last):
        ring_step(dgather, rd_send, rd_recv, s)
        for at in blocks_at(s):
            split_block(dgather, dsplit, at)
            columns = columns + column_term(dsplit, at)
    for i, peer in enumerate(w_peers):
        remote(mtop_ref, mtop4.at[peer], t_send.at[i], t_recv.at[peer], w_device(peer)).wait_recv()
        remote(btop_ref, btop4.at[peer], u_send.at[i], u_recv.at[peer], w_device(peer)).wait_recv()
        remote(masked.at[peer], data4.at[peer], w_send.at[i], w_recv.at[peer], w_device(peer)).wait_recv()
    topics = jnp.concatenate([mtop4[owner] for owner in range(NW)], axis=0)
    stacked = stack_topics(topics)
    acc = jnp.zeros((topics.shape[0], 2 * k), F32)
    for s in range(last):
        for at in blocks_at(s):
            acc = acc + block_term(stacked, data4, dsplit, at)
    ring_step(dgather, rd_send, rd_recv, last)
    for at in blocks_at(last):
        split_block(dgather, dsplit, at)
        columns = columns + column_term(dsplit, at)
        acc = acc + block_term(stacked, data4, dsplit, at)
    product, col_total = exchange(mpartial, 0, 0, acc, columns)
    topics = topics * product / col_total
    for i, peer in enumerate(z_peers):
        start(remote(data4.at[:, peer], data32.at[z], z_send.at[i], z_recv.at[z], z_device(peer)))
    data32[z] = data4[:, z]
    for update in range(1, UPDATES):
        acc = all_terms(stack_topics(topics), data4, dsplit)
        product, _ = exchange(mpartial, update, update, acc, None)
        topics = topics * product / col_total

    topics_z[z] = pack(topics)
    for i, peer in enumerate(z_peers):
        start(remote(topics_z.at[z], topics_z.at[z], g_send.at[i], g_recv.at[z], z_device(peer)))
    for i, peer in enumerate(w_peers):
        start(remote(bsend.at[peer], base4.at[w], b_send.at[i], b_recv.at[w], w_device(peer)))
    for i, peer in enumerate(z_peers):
        remote(data4.at[:, peer], data32.at[peer], z_send.at[i], z_recv.at[peer], z_device(peer)).wait_recv()
    for i, peer in enumerate(z_peers):
        remote(topics_z.at[z], topics_z.at[peer], g_send.at[i], g_recv.at[peer], z_device(peer)).wait_recv()
    rows = NW * docs
    every = jnp.concatenate([unpack(topics_z[at]) for at in range(nz)], axis=0)

    for at in range(nz):
        recon = dot(stack_topics(every[at * rows : (at + 1) * rows]), dsplit[z])
        data = jnp.concatenate([data32[at, owner] for owner in range(NW)], axis=0)
        high, low = split2(data / recon)
        for part, piece in enumerate((high, low, high)):
            q3[(part * nz + at) * rows : (part * nz + at + 1) * rows] = piece
    wide = turn_tall(every)
    high, low = split2(wide)
    numerator = dot(jnp.concatenate([high, high, low], axis=1), q3[...])
    new_dict = dgather[z] * numerator / jnp.sum(wide, axis=1, keepdims=True)

    onehot = (lax.broadcasted_iota(jnp.int32, (k, k), 0) == perm_ref[...]).astype(F32).astype(BF16)
    aligned = dot(
        jnp.concatenate(split3(turn_flat(new_dict)), axis=1), jnp.concatenate([onehot, onehot, onehot], axis=0)
    )
    for at in range(np_):
        p2_send[at] = pack(aligned[at * slab : (at + 1) * slab])
    for i, peer in enumerate(p_peers):
        start(remote(p2_send.at[peer], p2_recv.at[p], s_send.at[i], s_recv.at[p], p_device(peer)))
    p2_recv[p] = p2_send[p]
    for i, peer in enumerate(p_peers):
        remote(p2_send.at[peer], p2_recv.at[peer], s_send.at[i], s_recv.at[peer], p_device(peer)).wait_recv()
    median = middle([p2_recv[at] for at in range(np_)])
    p3_recv[p] = median
    for i, peer in enumerate(p_peers):
        start(remote(p3_recv.at[p], p3_recv.at[p], m_send.at[i], m_recv.at[p], p_device(peer)))
    med_ref[...] = unpack(median)
    for i, peer in enumerate(p_peers):
        remote(p3_recv.at[p], p3_recv.at[peer], m_send.at[i], m_recv.at[peer], p_device(peer)).wait_recv()

    mgather[z] = turn_tall(jnp.concatenate([unpack(p3_recv[at]) for at in range(np_)], axis=0))
    ring_first(mgather, rm_send, rm_recv)
    for i, peer in enumerate(w_peers):
        remote(bsend.at[peer], base4.at[peer], b_send.at[i], b_recv.at[peer], w_device(peer)).wait_recv()
    topics = jnp.concatenate([btop4[owner] for owner in range(NW)], axis=0)
    stacked = stack_topics(topics)
    acc = jnp.zeros((topics.shape[0], 2 * k), F32)
    columns = jnp.zeros((8, 2 * k), F32)
    for s in range(last + 1):
        if s < last:
            ring_step(mgather, rm_send, rm_recv, s + 1)
        for at in blocks_at(s):
            split_block(mgather, msplit, at)
            columns = columns + column_term(msplit, at)
            acc = acc + block_term(stacked, base4, msplit, at)
    product, col_total = exchange(bpartial, 0, UPDATES, acc, columns)
    topics = topics * product / col_total
    for update in range(1, REFITS):
        acc = all_terms(stack_topics(topics), base4, msplit)
        product, _ = exchange(bpartial, update, UPDATES + update, acc, None)
        topics = topics * product / col_total
    own = topics[0:bdocs]
    for owner in range(1, NW):
        own = jnp.where(w == owner, topics[owner * bdocs : (owner + 1) * bdocs], own)
    refit_ref[...] = own

    for copy in sends:
        copy.wait_send()


def per_device(counts, tile_mask, member_topics, start_dict, align_perm, base_counts, base_topics, *, np_, nz):
    docs, bdocs = counts.shape[1], base_counts.shape[0]
    wb, k = start_dict.shape[1:]
    slab = wb // np_
    last = nz // 2
    rows, brows = NW * docs, NW * bdocs
    sem = pltpu.SemaphoreType.DMA
    scratch = [
        pltpu.VMEM((NW, nz, docs, wb), F32),
        pltpu.VMEM((NW, nz, docs, wb), F32),
        pltpu.VMEM((nz, NW, docs, wb), F32),
        pltpu.VMEM((NW, nz, bdocs, wb), F32),
        pltpu.VMEM((NW, nz, bdocs, wb), F32),
        pltpu.VMEM((NW, docs, k), F32),
        pltpu.VMEM((NW, bdocs, k), F32),
        pltpu.VMEM((nz, k, wb), F32),
        pltpu.VMEM((nz, k, wb), F32),
        pltpu.VMEM((nz, 3 * k, wb), BF16),
        pltpu.VMEM((nz, 3 * k, wb), BF16),
        pltpu.VMEM((UPDATES, NW, rows // 2 + 8, 2 * k), F32),
        pltpu.VMEM((REFITS, NW, brows // 2 + 8, 2 * k), F32),
        pltpu.VMEM((nz, rows // 2, 2 * k), F32),
        pltpu.VMEM((3 * nz * rows, wb), BF16),
        pltpu.VMEM((np_, slab // 2, 2 * k), F32),
        pltpu.VMEM((np_, slab // 2, 2 * k), F32),
        pltpu.VMEM((np_, slab // 2, 2 * k), F32),
    ]
    for _ in range(4):
        scratch += [sem((NW - 1,)), sem((NW,))]
    for _ in range(2):
        scratch += [sem((2, last, 2)), sem((2, last, 2))]
    scratch += [sem((UPDATES + REFITS, NW - 1)), sem((UPDATES + REFITS, NW))]
    for _ in range(2):
        scratch += [sem((nz - 1,)), sem((nz,))]
    for _ in range(2):
        scratch += [sem((np_ - 1,)), sem((np_,))]
    vmem = pl.BlockSpec(memory_space=pltpu.VMEM)
    median, refit = pl.pallas_call(
        functools.partial(kernel, np_=np_, nz=nz),
        out_shape=(jax.ShapeDtypeStruct((slab, k), F32), jax.ShapeDtypeStruct((bdocs, k), F32)),
        in_specs=[vmem] * 7,
        out_specs=(vmem, vmem),
        scratch_shapes=scratch,
        compiler_params=pltpu.CompilerParams(
            collective_id=0, has_side_effects=True, vmem_limit_bytes=48 * 1024 * 1024
        ),
    )(counts[0], tile_mask[0], member_topics[0], start_dict[0], align_perm, base_counts, base_topics)
    return median[None, None], refit


def solution(mesh):
    np_ = mesh.shape["pert"]
    nz = mesh.shape["doc"] // NW
    return jax.shard_map(
        functools.partial(per_device, np_=np_, nz=nz),
        mesh=mesh,
        in_specs=(
            P("pert", "doc", None),
            P("pert", "doc", None),
            P("pert", "doc", None),
            P("pert", "doc", None),
            P("pert", None),
            P(("pert", "doc"), None),
            P(("pert", "doc"), None),
        ),
        out_specs=(P("doc", "pert", None, None), P(("pert", "doc"), None)),
        check_vma=False,
    )
```

time: 1210 us -> 101 us (0.08); the launches traced: 1190 us -> 101 us
  waiting for transfers between devices: 986 us -> 0 us
  Pallas kernels: 0 us -> 96.1 us
  blocking collectives: 78.6 us -> 0 us
  matrix products: 53.9 us -> 0 us
  other arithmetic: 46.3 us -> 0 us
  between operations: 14.1 us -> 0.72 us
    all_gather x2 -> x0, waiting for transfers between devices: 922 us -> none  [the longest x1 821 us: per_device(): joined = lax.all_gather(median_rows, ('pert', 'doc'), axis=0, tiled=True)]
    pallas_call x0 -> x1, Pallas kernels: none -> 96.1 us  [per_device(): pl.pallas_call(functools.partial(kernel, np_=np_, nz=nz), out_shape=(jax....]
    psum x1 -> x0, blocking collectives: 64.8 us -> none  [per_device(): topic_load = lax.psum(jnp.sum(topics, axis=0), 'doc')]
    reduce_scatter x1 -> x0, waiting for transfers between devices: 63.1 us -> none  [per_device(): lax.psum_scatter(lax.dot_general(quotient, topics, (((0,), (0,)), ((), ()...]
    dot_general x13 -> x0, matrix products: 53.9 us -> none  [the longest x6 24.8 us: recon_wide(): return jnp.dot(topics, dict_wide, precision=HIGHEST_PRECISION)]
    sort x1 -> x0, other arithmetic: 23.5 us -> none  [middle(): ordered = jnp.sort(stacked, axis=0)]
    reduce_sum x2 -> x0, other arithmetic: 21 us -> none  [the longest x1 18.5 us: per_device(): median_total = jnp.sum(median_wide, axis=1)]
    all_to_all x1 -> x0, blocking collectives: 13.8 us -> none  [per_device(): lax.all_to_all(aligned.reshape(members, sub_rows, topic_count), 'pert', s...]
  transfers between devices with their start and end apart: 3 -> 0, of which waited for: 3 -> 0; matrix products, arithmetic and copies ran while one was open for 0% -> 0% of each run, Pallas kernels for 0% -> 0%
where the time goes in v1:
time: 101 us
  Pallas kernels  96.1 us (95%)
  local copies, waits for them, and re-layouts  3.92 us (4%)
    pallas_call x1, Pallas kernels, per_device(): pl.pallas_call(functools.partial(kernel, np_=np_, nz=nz), out_shape=(jax....  96.1 us
    unnamed x15, local copies, waits for them, and re-layouts  3.92 us

profile of v1, /device:TPU:1, one launch (start us, length us, event | category | flops | bytes accessed | tf_op | source)
XLA Modules:
  0.0 100.8 jit_solution(8091120738219915128)
XLA Ops:
  0.6 0.0 copy-start.1
  0.6 0.0 copy-start.2
  0.7 0.0 copy-start.3
  0.7 0.0 copy-start.4
  0.7 1.1 %copy.9 = f32[1,512,64]{2,1,0:T(8,128)S(1)} copy(f32[1,512,64]{1,2,0:T(8,128)} %param.10) | data formatting | bytes 262144 | tf_op args[3]
  1.7 0.0 copy-start.5
  1.8 0.0 copy-done.1
  1.8 0.0 copy-done.2
  1.8 0.0 copy-done.3
  1.8 0.0 copy-done.4
  1.8 0.6 copy-done.5
  2.4 0.0 copy-start
  2.4 1.0 %copy-done = s32[1,8,16384]{2,1,0:T(8,128)S(1)} copy-done((s32[1,8,16384]{2,1,0:T(8,128)S(1)}, s32[1,8,16384]{2,1,0:T(8,128)}, u32[]{:S(2)}) %copy-start) | copy-done | bytes 524312
  3.4 96.1 %shard_map.86 = (f32[32,64]{1,0:T(8,128)S(1)}, f32[4,64]{1,0:T(4,128)S(1)}) custom-call(s32[8,16384]{1,0:T(8,128)S(1)} %bitcast.6, s32[8,128]{1,0:T(8,128)S(1)} %bitcast.8, f32[8,64]{1,0:T(8,128)S(1)} %bitcast.9, f32[512,64]{1,0:T(8,128)S(1)} %bitcast.5, s32[1,64]{1,0:T(1,128)S(1)} %copy-done.5, s32[4,16384]{1,0:T(4,128)S(1)} %copy-done.1, f32[4,64]{1,0:T(4,128)S(1)} %copy-done.4), custom_call_target="tpu_custom_call" | custom-call | tf_op jit(solution)/shard_map/pallas_call | solution.py:399
  99.6 0.6 copy.12
  100.2 0.6 copy.13
Async XLA Ops:
  0.6 1.1 %copy-start.1 = (s32[4,16384]{1,0:T(4,128)S(1)}, s32[4,16384]{1,0:T(4,128)}, u32[]{:S(2)}) copy-start(s32[4,16384]{1,0:T(4,128)} %base_ref.1) | copy-start | bytes 786436
  0.6 1.1 %copy-start.2 = (s32[1,8,128]{2,1,0:T(8,128)S(1)}, s32[1,8,128]{2,1,0:T(8,128)}, u32[]{:S(2)}) copy-start(s32[1,8,128]{2,1,0:T(8,128)} %param.8) | copy-start | bytes 12292
  0.7 1.1 %copy-start.3 = (f32[1,8,64]{2,1,0:T(8,128)S(1)}, f32[1,8,64]{2,1,0:T(8,128)}, u32[]{:S(2)}) copy-start(f32[1,8,64]{2,1,0:T(8,128)} %param.9) | copy-start | bytes 6148
  0.7 1.1 %copy-start.4 = (f32[4,64]{1,0:T(4,128)S(1)}, f32[4,64]{1,0:T(4,128)}, u32[]{:S(2)}) copy-start(f32[4,64]{1,0:T(4,128)} %btop_ref.1) | copy-start | bytes 3076
  1.7 0.7 copy-start.5
  2.4 1.0 %copy-start = (s32[1,8,16384]{2,1,0:T(8,128)S(1)}, s32[1,8,16384]{2,1,0:T(8,128)}, u32[]{:S(2)}) copy-start(s32[1,8,16384]{2,1,0:T(8,128)} %param.7) | copy-start | bytes 1572868

commit v2 on v1

v2 whole, which is shorter than its diff:
```python
import functools

import jax
import jax.numpy as jnp
from jax import lax
from jax.experimental import pallas as pl
from jax.experimental.pallas import tpu as pltpu
from jax.sharding import PartitionSpec as P

UPDATES = 3
REFITS = 2
NX = 2
NC = 2
NW = NX * NC
MESH = pl.DeviceIdType.MESH
F32 = jnp.float32
BF16 = jnp.bfloat16


def sort_pairs(count):
    pairs = []
    span = 1
    while span < count:
        step = span
        while step >= 1:
            for start in range(step % span, count - step, 2 * step):
                for at in range(min(step, count - start - step)):
                    low, high = start + at, start + at + step
                    if low // (2 * span) == high // (2 * span):
                        pairs.append((low, high))
            step //= 2
        span *= 2
    return pairs


def middle(rows):
    rows = list(rows)
    for low, high in sort_pairs(len(rows)):
        rows[low], rows[high] = jnp.minimum(rows[low], rows[high]), jnp.maximum(rows[low], rows[high])
    at = len(rows) // 2
    return 0.5 * (rows[at - 1] + rows[at])


def split2(x):
    high = x.astype(BF16)
    return high, (x - high.astype(F32)).astype(BF16)


def split3(x):
    high = x.astype(BF16)
    rest = x - high.astype(F32)
    mid = rest.astype(BF16)
    return high, mid, (rest - mid.astype(F32)).astype(BF16)


def pack(x):
    half = x.shape[0] // 2
    return jnp.concatenate([x[:half], x[half:]], axis=1)


def unpack(x):
    half = x.shape[1] // 2
    return jnp.concatenate([x[:, :half], x[:, half:]], axis=0)


def turn_tall(x):
    wide = jnp.concatenate([x, jnp.zeros_like(x)], axis=1)
    return wide.T[: x.shape[1]]


def turn_flat(x):
    tall = jnp.concatenate([x, jnp.zeros_like(x)], axis=0)
    return tall.T[:, : x.shape[0]]


def dot(a, b):
    return jnp.dot(a, b, preferred_element_type=F32)


def dot_nt(a, b):
    return lax.dot_general(a, b, (((1,), (1,)), ((), ())), preferred_element_type=F32)


def kernel(
    counts_ref, mask_ref, mtop_ref, dict_ref, perm_ref, base_ref, btop_ref,
    med_ref, refit_ref,
    counts_in, mask_in, perm_in, base_in,
    masked, data4, data32, bsend, base8, bdata, mtop4, btop8, dgather, mgather, dsplit, msplit,
    mpartial, bpartial, topics_z, q3, p2_send, p2_recv, p3_recv, in_sem,
    w_send, w_recv, t_send, t_recv, x_send, x_recv, a_send, a_recv, r_send, r_recv,
    z_send, z_recv, g_send, g_recv, b_send, b_recv, u_send, u_recv, e_send, e_recv, s_send, s_recv, m_send, m_recv,
    *, np_, nz,
):
    k, wb = dict_ref.shape
    docs, bdocs = mtop_ref.shape[0], btop_ref.shape[0]
    p = lax.axis_index("pert")
    b = lax.axis_index("doc")
    xh, z, c = b // (nz * NC), (b // NC) % nz, b % NC
    w = xh * NC + c
    chunk = k // 2
    slab = wb // np_

    def w_device(at):
        return (p, (at // NC) * (nz * NC) + z * NC + at % NC)

    def z_device(at):
        return (p, xh * (nz * NC) + at * NC + c)

    def p_device(at):
        return (at, b)

    w_peers = [lax.rem(w + i, NW) for i in range(1, NW)]
    z_peers = [lax.rem(z + i, nz) for i in range(1, nz)]
    p_peers = [lax.rem(p + i, np_) for i in range(1, np_)]

    loads = [
        pltpu.make_async_copy(src, dst, in_sem.at[i])
        for i, (src, dst) in enumerate(
            (
                (mask_ref, mask_in),
                (counts_ref, counts_in),
                (dict_ref, dgather.at[z]),
                (base_ref, base_in),
                (mtop_ref, mtop4.at[w]),
                (btop_ref, btop8.at[z]),
                (perm_ref, perm_in),
            )
        )
    ]
    for load in loads:
        load.start()

    barrier = pltpu.get_barrier_semaphore()
    for peer in w_peers:
        pl.semaphore_signal(barrier, inc=1, device_id=w_device(peer), device_id_type=MESH)
    for peer in z_peers:
        pl.semaphore_signal(barrier, inc=1, device_id=z_device(peer), device_id_type=MESH)
    for peer in p_peers:
        pl.semaphore_signal(barrier, inc=1, device_id=p_device(peer), device_id_type=MESH)

    for load in loads:
        load.wait()
    tiles = mask_ref.shape[1]
    tile_width = counts_ref.shape[1] // tiles
    per_block = wb // tile_width
    tile_ids = lax.broadcasted_iota(jnp.int32, (docs, tiles), 1)
    doc_ids = b * docs + lax.broadcasted_iota(jnp.int32, (docs, tiles), 0)
    occupied = jnp.maximum(mask_in[...], (tile_ids == doc_ids % tiles).astype(jnp.int32)).astype(F32)

    for owner in range(NW):

        def mask_block(zb, carry, owner=owner):
            block = ((owner // NC) * nz + zb) * NC + owner % NC
            for j in range(per_block):
                tile = block * per_block + j
                seen = jnp.sum(jnp.where(tile_ids == tile, occupied, 0.0), axis=1, keepdims=True)
                at = pl.multiple_of(tile * tile_width, tile_width)
                masked[owner, zb, :, j * tile_width : (j + 1) * tile_width] = (
                    counts_in[:, pl.ds(at, tile_width)].astype(F32) * seen
                )
            at = pl.multiple_of(block * wb, wb)
            bsend[owner, zb] = base_in[:, pl.ds(at, wb)].astype(F32)
            return carry

        lax.fori_loop(0, nz, mask_block, 0)

    pl.semaphore_wait(barrier, NW - 1 + nz - 1 + np_ - 1)

    sends = []

    def remote(src, dst, ssem, rsem, device):
        return pltpu.make_async_remote_copy(
            src_ref=src, dst_ref=dst, send_sem=ssem, recv_sem=rsem, device_id=device, device_id_type=MESH
        )

    def start(copy):
        copy.start()
        sends.append(copy)

    last = nz // 2

    def ring_block(way, far):
        return lax.rem(z + nz - far, nz) if way == 0 else lax.rem(z + far, nz)

    def ring_copy(way, far, ch, hops):
        at = dgather.at[ring_block(way, far), pl.ds(ch * chunk, chunk), :]
        number = far + hops - 1
        return remote(
            at, at, r_send.at[way, number, ch], r_recv.at[way, number, ch], z_device(ring_block(1 - way, hops))
        )

    def ring_first():
        for ch in (0, 1):
            for way in (0, 1):
                start(ring_copy(way, 0, ch, 1))

    def ring_step(far):
        for ch in (0, 1):
            for way in (0, 1):
                if far == last and ch != way:
                    continue
                here = dgather.at[ring_block(way, far), pl.ds(ch * chunk, chunk), :]
                remote(
                    here, here, r_send.at[way, far - 1, ch], r_recv.at[way, far - 1, ch], z_device(ring_block(1 - way, 1))
                ).wait_recv()
                if far == last - 2 and ch == way:
                    start(ring_copy(way, far, ch, 2))
                if far < last - 1:
                    start(ring_copy(way, far, ch, 1))

    def blocks_at(far):
        if far == 0 or far == last:
            return [ring_block(0, far)]
        return [ring_block(0, far), ring_block(1, far)]

    def split_block(buf, out, at):
        high, low = split2(buf[at])
        out[at, 0:k] = high
        out[at, k : 2 * k] = low
        out[at, 2 * k : 3 * k] = high

    def stack_topics(topics):
        high, low = split2(topics)
        return jnp.concatenate([high, high, low], axis=1)

    def rows_of(at):
        return jnp.concatenate([data4[owner, at] for owner in range(NW)], axis=0)

    def block_term(stacked, data, split, at):
        rows = data.shape[0]
        high, low = split2(data / dot(stacked, split[at]))
        both = dot_nt(jnp.concatenate([high, low], axis=0), split[at, 0 : 2 * k])
        return both[:rows] + both[rows:]

    def column_term(split, at):
        return dot_nt(jnp.ones((16, wb), BF16), split[at, 0 : 2 * k])[:8]

    def fold(x):
        return x[:, :k] + x[:, k:]

    def exchange(partial, at, me, peers, device, sems, acc, columns, meanwhile=None):
        rows = acc.shape[0] // 2
        partial[at, me, 0:rows] = pack(fold(acc))
        sent = rows
        if columns is not None:
            partial[at, me, rows : rows + 8] = columns
            sent = rows + 8
        ssem, rsem = sems
        for i, peer in enumerate(peers):
            mine = partial.at[at, me, 0:sent]
            start(remote(mine, mine, ssem.at[at, i], rsem.at[at, me], device(peer)))
        if meanwhile is not None:
            meanwhile()
        for i, peer in enumerate(peers):
            theirs = partial.at[at, peer, 0:sent]
            remote(theirs, theirs, ssem.at[at, i], rsem.at[at, peer], device(peer)).wait_recv()
        total = partial[at, 0, 0:sent]
        for owner in range(1, len(peers) + 1):
            total = total + partial[at, owner, 0:sent]
        product = unpack(total[:rows])
        return product, (fold(total[rows : rows + 1]) if columns is not None else None)

    ring_first()
    for i, peer in enumerate(w_peers):
        start(remote(masked.at[peer], data4.at[w], w_send.at[i], w_recv.at[w], w_device(peer)))
        start(remote(mtop4.at[w], mtop4.at[w], t_send.at[i], t_recv.at[w], w_device(peer)))
    data4[w] = masked[w]
    split_block(dgather, dsplit, z)
    columns = column_term(dsplit, z)

    for far in range(1, last - 1):
        ring_step(far)
        for at in blocks_at(far):
            split_block(dgather, dsplit, at)
            columns = columns + column_term(dsplit, at)
    for i, peer in enumerate(w_peers):
        remote(mtop4.at[w], mtop4.at[peer], t_send.at[i], t_recv.at[peer], w_device(peer)).wait_recv()
        remote(masked.at[peer], data4.at[peer], w_send.at[i], w_recv.at[peer], w_device(peer)).wait_recv()
    topics = jnp.concatenate([mtop4[owner] for owner in range(NW)], axis=0)
    stacked = stack_topics(topics)
    acc = jnp.zeros((topics.shape[0], 2 * k), F32)
    for far in range(last - 1):
        for at in blocks_at(far):
            acc = acc + block_term(stacked, rows_of(at), dsplit, at)
    for far in range(last - 1, last + 1):
        ring_step(far)
        for at in blocks_at(far):
            split_block(dgather, dsplit, at)
            columns = columns + column_term(dsplit, at)
            acc = acc + block_term(stacked, rows_of(at), dsplit, at)

    def own_words():
        for i, peer in enumerate(z_peers):
            start(remote(data4.at[:, peer], data32.at[z], z_send.at[i], z_recv.at[z], z_device(peer)))
        data32[z] = data4[:, z]

    product, col_total = exchange(mpartial, 0, w, w_peers, w_device, (a_send, a_recv), acc, columns, own_words)
    topics = topics * product / col_total
    for update in range(1, UPDATES):
        stacked = stack_topics(topics)
        acc = sum(block_term(stacked, rows_of(at), dsplit, at) for at in range(nz))
        product, _ = exchange(mpartial, update, w, w_peers, w_device, (a_send, a_recv), acc, None)
        topics = topics * product / col_total

    topics_z[z] = pack(topics)
    for i, peer in enumerate(z_peers):
        start(remote(topics_z.at[z], topics_z.at[z], g_send.at[i], g_recv.at[z], z_device(peer)))
    for i, peer in enumerate(z_peers):
        remote(topics_z.at[z], topics_z.at[peer], g_send.at[i], g_recv.at[peer], z_device(peer)).wait_recv()
    for i, peer in enumerate(z_peers):
        remote(data4.at[:, peer], data32.at[peer], z_send.at[i], z_recv.at[peer], z_device(peer)).wait_recv()
    for i, peer in enumerate(z_peers):
        start(remote(bsend.at[:, peer], base8.at[z], b_send.at[i], b_recv.at[z], z_device(peer)))
        start(remote(btop8.at[z], btop8.at[z], u_send.at[i], u_recv.at[z], z_device(peer)))
    base8[z] = bsend[:, z]
    rows = NW * docs
    every = jnp.concatenate([unpack(topics_z[at]) for at in range(nz)], axis=0)

    for at in range(nz):
        recon = dot(stack_topics(every[at * rows : (at + 1) * rows]), dsplit[z])
        data = jnp.concatenate([data32[at, owner] for owner in range(NW)], axis=0)
        high, low = split2(data / recon)
        for part, piece in enumerate((high, low, high)):
            q3[(part * nz + at) * rows : (part * nz + at + 1) * rows] = piece
    wide = turn_tall(every)
    high, low = split2(wide)
    numerator = dot(jnp.concatenate([high, high, low], axis=1), q3[...])
    new_dict = dgather[z] * numerator / jnp.sum(wide, axis=1, keepdims=True)

    onehot = (lax.broadcasted_iota(jnp.int32, (k, k), 0) == perm_in[...]).astype(F32).astype(BF16)
    aligned = dot(
        jnp.concatenate(split3(turn_flat(new_dict)), axis=1), jnp.concatenate([onehot, onehot, onehot], axis=0)
    )
    for at in range(np_):
        p2_send[at] = pack(aligned[at * slab : (at + 1) * slab])
    for i, peer in enumerate(p_peers):
        start(remote(p2_send.at[peer], p2_recv.at[p], s_send.at[i], s_recv.at[p], p_device(peer)))
    p2_recv[p] = p2_send[p]
    for i, peer in enumerate(z_peers):
        remote(bsend.at[:, peer], base8.at[peer], b_send.at[i], b_recv.at[peer], z_device(peer)).wait_recv()
        remote(btop8.at[z], btop8.at[peer], u_send.at[i], u_recv.at[peer], z_device(peer)).wait_recv()
    for owner in range(NW):
        bdata[owner] = jnp.concatenate([base8[at, owner] for at in range(nz)], axis=0)
    topics = jnp.concatenate([btop8[at] for at in range(nz)], axis=0)
    stacked = stack_topics(topics)
    for i, peer in enumerate(p_peers):
        remote(p2_send.at[peer], p2_recv.at[peer], s_send.at[i], s_recv.at[peer], p_device(peer)).wait_recv()
    median = middle([p2_recv[at] for at in range(np_)])
    p3_recv[p] = median
    for i, peer in enumerate(p_peers):
        start(remote(p3_recv.at[p], p3_recv.at[p], m_send.at[i], m_recv.at[p], p_device(peer)))
    med_ref[...] = unpack(median)
    for i, peer in enumerate(p_peers):
        remote(p3_recv.at[p], p3_recv.at[peer], m_send.at[i], m_recv.at[peer], p_device(peer)).wait_recv()

    mgather[w] = turn_tall(jnp.concatenate([unpack(p3_recv[at]) for at in range(np_)], axis=0))
    for i, peer in enumerate(w_peers):
        start(remote(mgather.at[w], mgather.at[w], x_send.at[i], x_recv.at[w], w_device(peer)))
    split_block(mgather, msplit, w)
    columns = column_term(msplit, w)
    acc = block_term(stacked, bdata[w], msplit, w)
    for i, peer in enumerate(w_peers):
        remote(mgather.at[w], mgather.at[peer], x_send.at[i], x_recv.at[peer], w_device(peer)).wait_recv()
        split_block(mgather, msplit, peer)
        columns = columns + column_term(msplit, peer)
        acc = acc + block_term(stacked, bdata[peer], msplit, peer)
    product, col_total = exchange(bpartial, 0, z, z_peers, z_device, (e_send, e_recv), acc, columns)
    topics = topics * product / col_total
    for update in range(1, REFITS):
        stacked = stack_topics(topics)
        acc = sum(block_term(stacked, bdata[at], msplit, at) for at in range(NW))
        product, _ = exchange(bpartial, update, z, z_peers, z_device, (e_send, e_recv), acc, None)
        topics = topics * product / col_total
    own = topics[0:bdocs]
    for at in range(1, nz):
        own = jnp.where(z == at, topics[at * bdocs : (at + 1) * bdocs], own)
    refit_ref[...] = own

    for copy in sends:
        copy.wait_send()


def per_device(counts, tile_mask, member_topics, start_dict, align_perm, base_counts, base_topics, *, np_, nz):
    docs, bdocs = counts.shape[1], base_counts.shape[0]
    wb, k = start_dict.shape[1:]
    slab = wb // np_
    last = nz // 2
    rows, brows = NW * docs, nz * bdocs
    sem = pltpu.SemaphoreType.DMA
    scratch = [
        pltpu.VMEM(counts.shape[1:], counts.dtype),
        pltpu.VMEM(tile_mask.shape[1:], tile_mask.dtype),
        pltpu.VMEM(align_perm.shape, align_perm.dtype),
        pltpu.VMEM(base_counts.shape, base_counts.dtype),
        pltpu.VMEM((NW, nz, docs, wb), F32),
        pltpu.VMEM((NW, nz, docs, wb), F32),
        pltpu.VMEM((nz, NW, docs, wb), F32),
        pltpu.VMEM((NW, nz, bdocs, wb), F32),
        pltpu.VMEM((nz, NW, bdocs, wb), F32),
        pltpu.VMEM((NW, brows, wb), F32),
        pltpu.VMEM((NW, docs, k), F32),
        pltpu.VMEM((nz, bdocs, k), F32),
        pltpu.VMEM((nz, k, wb), F32),
        pltpu.VMEM((NW, k, wb), F32),
        pltpu.VMEM((nz, 3 * k, wb), BF16),
        pltpu.VMEM((NW, 3 * k, wb), BF16),
        pltpu.VMEM((UPDATES, NW, rows // 2 + 8, 2 * k), F32),
        pltpu.VMEM((REFITS, nz, brows // 2 + 8, 2 * k), F32),
        pltpu.VMEM((nz, rows // 2, 2 * k), F32),
        pltpu.VMEM((3 * nz * rows, wb), BF16),
        pltpu.VMEM((np_, slab // 2, 2 * k), F32),
        pltpu.VMEM((np_, slab // 2, 2 * k), F32),
        pltpu.VMEM((np_, slab // 2, 2 * k), F32),
        sem((7,)),
    ]
    for _ in range(3):
        scratch += [sem((NW - 1,)), sem((NW,))]
    scratch += [sem((UPDATES, NW - 1)), sem((UPDATES, NW))]
    scratch += [sem((2, last, 2)), sem((2, last, 2))]
    for _ in range(4):
        scratch += [sem((nz - 1,)), sem((nz,))]
    scratch += [sem((REFITS, nz - 1)), sem((REFITS, nz))]
    for _ in range(2):
        scratch += [sem((np_ - 1,)), sem((np_,))]
    here = pl.BlockSpec(memory_space=pl.ANY)
    vmem = pl.BlockSpec(memory_space=pltpu.VMEM)
    median, refit = pl.pallas_call(
        functools.partial(kernel, np_=np_, nz=nz),
        out_shape=(jax.ShapeDtypeStruct((slab, k), F32), jax.ShapeDtypeStruct((bdocs, k), F32)),
        in_specs=[here] * 7,
        out_specs=(vmem, vmem),
        scratch_shapes=scratch,
        compiler_params=pltpu.CompilerParams(collective_id=0, has_side_effects=True),
    )(counts[0], tile_mask[0], member_topics[0], start_dict[0].T, align_perm, base_counts, base_topics)
    return median[None, None], refit


def solution(mesh):
    np_ = mesh.shape["pert"]
    nz = mesh.shape["doc"] // NW
    return jax.shard_map(
        functools.partial(per_device, np_=np_, nz=nz),
        mesh=mesh,
        in_specs=(
            P("pert", "doc", None),
            P("pert", "doc", None),
            P("pert", "doc", None),
            P("pert", "doc", None),
            P("pert", None),
            P(("pert", "doc"), None),
            P(("pert", "doc"), None),
        ),
        out_specs=(P("doc", "pert", None, None), P(("pert", "doc"), None)),
        check_vma=False,
    )
```

time: 101 us -> 89.5 us (0.89)
  Pallas kernels: 96.1 us -> 86.8 us
  local copies, waits for them, and re-layouts: 3.92 us -> 1.91 us
    pallas_call x1, Pallas kernels: 96.1 us -> 86.8 us  [per_device(): pl.pallas_call(functools.partial(kernel, np_=np_, nz=nz), out_shape=(jax....]
    unnamed x15 -> x4, local copies, waits for them, and re-layouts: 3.92 us -> 1.91 us
where the time goes in v2:
time: 89.5 us; the launch traced here: 89.3 us
  Pallas kernels  86.8 us (97%)
  local copies, waits for them, and re-layouts  1.91 us (2%)
    pallas_call x1, Pallas kernels, per_device(): pl.pallas_call(functools.partial(kernel, np_=np_, nz=nz), out_shape=(jax....  86.8 us
    unnamed x4, local copies, waits for them, and re-layouts  1.91 us

profile of v2, /device:TPU:1, one launch (start us, length us, event | category | flops | bytes accessed | tf_op | source)
XLA Modules:
  0.0 89.3 jit_solution(12404029688735670400)
XLA Ops:
  0.6 86.8 %shard_map.86 = (f32[32,64]{1,0:T(8,128)}, f32[4,64]{1,0:T(4,128)}) custom-call(s32[8,16384]{1,0:T(8,128)} %bitcast.7, s32[8,128]{1,0:T(8,128)} %bitcast.10, f32[8,64]{1,0:T(8,128)} %bitcast.11, f32[64,512]{1,0:T(8,128)} %bitcast.8, s32[1,64]{1,0:T(1,128)} %perm_ref.1, s32[4,16384]{1,0:T(4,128)} %base_ref.1, f32[4,64]{1,0:T(4,128)} %btop_ref.1), custom_call_target="tpu_custom_call" | custom-call | tf_op jit(solution)/shard_map/pallas_call | solution.py:427
  87.4 0.0 copy-start
  87.4 1.3 %copy.11 = f32[1,1,32,64]{3,2,1,0:T(8,128)} copy(f32[1,1,32,64]{3,2,1,0:T(8,128)} %bitcast.9) | data formatting | bytes 16384
  88.7 0.0 copy-done
  88.7 0.6 copy.12
Async XLA Ops:
  87.4 1.3 %copy-start = (f32[4,64]{1,0:T(4,128)S(1)}, f32[4,64]{1,0:T(4,128)}, u32[]{:S(2)}) copy-start(f32[4,64]{1,0:T(4,128)} %get-tuple-element.9) | copy-start | bytes 3076

commit v3 on v2

--- a/solution.py
+++ b/solution.py
@@ -97,7 +97,7 @@
     b = lax.axis_index("doc")
     xh, z, c = b // (nz * NC), (b // NC) % nz, b % NC
     w = xh * NC + c
-    chunk = k // 2
+    chunk = k // 4
     slab = wb // np_
 
     def w_device(at):
@@ -117,9 +117,9 @@
         pltpu.make_async_copy(src, dst, in_sem.at[i])
         for i, (src, dst) in enumerate(
             (
+                (dict_ref, dgather.at[z]),
                 (mask_ref, mask_in),
                 (counts_ref, counts_in),
-                (dict_ref, dgather.at[z]),
                 (base_ref, base_in),
                 (mtop_ref, mtop4.at[w]),
                 (btop_ref, btop8.at[z]),
@@ -138,32 +138,7 @@
     for peer in p_peers:
         pl.semaphore_signal(barrier, inc=1, device_id=p_device(peer), device_id_type=MESH)
 
-    for load in loads:
-        load.wait()
-    tiles = mask_ref.shape[1]
-    tile_width = counts_ref.shape[1] // tiles
-    per_block = wb // tile_width
-    tile_ids = lax.broadcasted_iota(jnp.int32, (docs, tiles), 1)
-    doc_ids = b * docs + lax.broadcasted_iota(jnp.int32, (docs, tiles), 0)
-    occupied = jnp.maximum(mask_in[...], (tile_ids == doc_ids % tiles).astype(jnp.int32)).astype(F32)
-
-    for owner in range(NW):
-
-        def mask_block(zb, carry, owner=owner):
-            block = ((owner // NC) * nz + zb) * NC + owner % NC
-            for j in range(per_block):
-                tile = block * per_block + j
-                seen = jnp.sum(jnp.where(tile_ids == tile, occupied, 0.0), axis=1, keepdims=True)
-                at = pl.multiple_of(tile * tile_width, tile_width)
-                masked[owner, zb, :, j * tile_width : (j + 1) * tile_width] = (
-                    counts_in[:, pl.ds(at, tile_width)].astype(F32) * seen
-                )
-            at = pl.multiple_of(block * wb, wb)
-            bsend[owner, zb] = base_in[:, pl.ds(at, wb)].astype(F32)
-            return carry
-
-        lax.fori_loop(0, nz, mask_block, 0)
-
+    loads[0].wait()
     pl.semaphore_wait(barrier, NW - 1 + nz - 1 + np_ - 1)
 
     sends = []
@@ -190,20 +165,20 @@
         )
 
     def ring_first():
-        for ch in (0, 1):
+        for ch in range(4):
             for way in (0, 1):
                 start(ring_copy(way, 0, ch, 1))
 
     def ring_step(far):
-        for ch in (0, 1):
+        for ch in range(4):
             for way in (0, 1):
-                if far == last and ch != way:
+                if far == last and ch // 2 != way:
                     continue
                 here = dgather.at[ring_block(way, far), pl.ds(ch * chunk, chunk), :]
                 remote(
                     here, here, r_send.at[way, far - 1, ch], r_recv.at[way, far - 1, ch], z_device(ring_block(1 - way, 1))
                 ).wait_recv()
-                if far == last - 2 and ch == way:
+                if far == last - 2 and ch // 2 == way:
                     start(ring_copy(way, far, ch, 2))
                 if far < last - 1:
                     start(ring_copy(way, far, ch, 1))
@@ -261,18 +236,43 @@
         return product, (fold(total[rows : rows + 1]) if columns is not None else None)
 
     ring_first()
+    for load in loads[1:]:
+        load.wait()
+    tiles = mask_ref.shape[1]
+    tile_width = counts_ref.shape[1] // tiles
+    per_block = wb // tile_width
+    tile_ids = lax.broadcasted_iota(jnp.int32, (docs, tiles), 1)
+    doc_ids = b * docs + lax.broadcasted_iota(jnp.int32, (docs, tiles), 0)
+    occupied = jnp.maximum(mask_in[...], (tile_ids == doc_ids % tiles).astype(jnp.int32)).astype(F32)
+
+    for owner in range(NW):
+
+        def mask_block(zb, carry, owner=owner):
+            block = ((owner // NC) * nz + zb) * NC + owner % NC
+            for j in range(per_block):
+                tile = block * per_block + j
+                seen = jnp.sum(jnp.where(tile_ids == tile, occupied, 0.0), axis=1, keepdims=True)
+                at = pl.multiple_of(tile * tile_width, tile_width)
+                masked[owner, zb, :, j * tile_width : (j + 1) * tile_width] = (
+                    counts_in[:, pl.ds(at, tile_width)].astype(F32) * seen
+                )
+            at = pl.multiple_of(block * wb, wb)
+            bsend[owner, zb] = base_in[:, pl.ds(at, wb)].astype(F32)
+            return carry
+
+        lax.fori_loop(0, nz, mask_block, 0)
     for i, peer in enumerate(w_peers):
         start(remote(masked.at[peer], data4.at[w], w_send.at[i], w_recv.at[w], w_device(peer)))
         start(remote(mtop4.at[w], mtop4.at[w], t_send.at[i], t_recv.at[w], w_device(peer)))
-    data4[w] = masked[w]
-    split_block(dgather, dsplit, z)
-    columns = column_term(dsplit, z)
-
     for far in range(1, last - 1):
         ring_step(far)
+    data4[w] = masked[w]
+    columns = jnp.zeros((8, 2 * k), F32)
+    for far in range(last - 1):
         for at in blocks_at(far):
             split_block(dgather, dsplit, at)
             columns = columns + column_term(dsplit, at)
+
     for i, peer in enumerate(w_peers):
         remote(mtop4.at[w], mtop4.at[peer], t_send.at[i], t_recv.at[peer], w_device(peer)).wait_recv()
         remote(masked.at[peer], data4.at[peer], w_send.at[i], w_recv.at[peer], w_device(peer)).wait_recv()
@@ -336,6 +336,13 @@
     for i, peer in enumerate(p_peers):
         start(remote(p2_send.at[peer], p2_recv.at[p], s_send.at[i], s_recv.at[p], p_device(peer)))
     p2_recv[p] = p2_send[p]
+    for i, peer in enumerate(p_peers):
+        remote(p2_send.at[peer], p2_recv.at[peer], s_send.at[i], s_recv.at[peer], p_device(peer)).wait_recv()
+    median = middle([p2_recv[at] for at in range(np_)])
+    p3_recv[p] = median
+    for i, peer in enumerate(p_peers):
+        start(remote(p3_recv.at[p], p3_recv.at[p], m_send.at[i], m_recv.at[p], p_device(peer)))
+    med_ref[...] = unpack(median)
     for i, peer in enumerate(z_peers):
         remote(bsend.at[:, peer], base8.at[peer], b_send.at[i], b_recv.at[peer], z_device(peer)).wait_recv()
         remote(btop8.at[z], btop8.at[peer], u_send.at[i], u_recv.at[peer], z_device(peer)).wait_recv()
@@ -343,13 +350,6 @@
         bdata[owner] = jnp.concatenate([base8[at, owner] for at in range(nz)], axis=0)
     topics = jnp.concatenate([btop8[at] for at in range(nz)], axis=0)
     stacked = stack_topics(topics)
-    for i, peer in enumerate(p_peers):
-        remote(p2_send.at[peer], p2_recv.at[peer], s_send.at[i], s_recv.at[peer], p_device(peer)).wait_recv()
-    median = middle([p2_recv[at] for at in range(np_)])
-    p3_recv[p] = median
-    for i, peer in enumerate(p_peers):
-        start(remote(p3_recv.at[p], p3_recv.at[p], m_send.at[i], m_recv.at[p], p_device(peer)))
-    med_ref[...] = unpack(median)
     for i, peer in enumerate(p_peers):
         remote(p3_recv.at[p], p3_recv.at[peer], m_send.at[i], m_recv.at[peer], p_device(peer)).wait_recv()
 
@@ -416,7 +416,7 @@
     for _ in range(3):
         scratch += [sem((NW - 1,)), sem((NW,))]
     scratch += [sem((UPDATES, NW - 1)), sem((UPDATES, NW))]
-    scratch += [sem((2, last, 2)), sem((2, last, 2))]
+    scratch += [sem((2, last, 4)), sem((2, last, 4))]
     for _ in range(4):
         scratch += [sem((nz - 1,)), sem((nz,))]
     scratch += [sem((REFITS, nz - 1)), sem((REFITS, nz))]

time: 89.5 us -> 84.7 us (0.946)
  Pallas kernels: 86.8 us -> 81.9 us
    pallas_call x1, Pallas kernels: 86.8 us -> 81.9 us  [per_device(): pl.pallas_call(functools.partial(kernel, np_=np_, nz=nz), out_shape=(jax....]
where the time goes in v3:
time: 84.7 us; the launch traced here: 84.5 us
  Pallas kernels  81.9 us (97%)
  local copies, waits for them, and re-layouts  1.91 us (2%)
    pallas_call x1, Pallas kernels, per_device(): pl.pallas_call(functools.partial(kernel, np_=np_, nz=nz), out_shape=(jax....  81.9 us
    unnamed x4, local copies, waits for them, and re-layouts  1.91 us

profile of v3, /device:TPU:1, one launch (start us, length us, event | category | flops | bytes accessed | tf_op | source)
XLA Modules:
  0.0 84.5 jit_solution(5021996650141487717)
XLA Ops:
  0.6 81.9 %shard_map.86 = (f32[32,64]{1,0:T(8,128)}, f32[4,64]{1,0:T(4,128)}) custom-call(s32[8,16384]{1,0:T(8,128)} %bitcast.7, s32[8,128]{1,0:T(8,128)} %bitcast.10, f32[8,64]{1,0:T(8,128)} %bitcast.11, f32[64,512]{1,0:T(8,128)} %bitcast.8, s32[1,64]{1,0:T(1,128)} %perm_ref.1, s32[4,16384]{1,0:T(4,128)} %base_ref.1, f32[4,64]{1,0:T(4,128)} %btop_ref.1), custom_call_target="tpu_custom_call" | custom-call | tf_op jit(solution)/shard_map/pallas_call | solution.py:427
  82.6 0.0 copy-start
  82.6 1.3 %copy.11 = f32[1,1,32,64]{3,2,1,0:T(8,128)} copy(f32[1,1,32,64]{3,2,1,0:T(8,128)} %bitcast.9) | data formatting | bytes 16384
  83.9 0.0 copy-done
  83.9 0.6 copy.12
Async XLA Ops:
  82.6 1.3 %copy-start = (f32[4,64]{1,0:T(4,128)S(1)}, f32[4,64]{1,0:T(4,128)}, u32[]{:S(2)}) copy-start(f32[4,64]{1,0:T(4,128)} %get-tuple-element.9) | copy-start | bytes 3076

commit v4 on v3

--- a/solution.py
+++ b/solution.py
@@ -86,7 +86,7 @@
     med_ref, refit_ref,
     counts_in, mask_in, perm_in, base_in,
     masked, data4, data32, bsend, base8, bdata, mtop4, btop8, dgather, mgather, dsplit, msplit,
-    mpartial, bpartial, topics_z, q3, p2_send, p2_recv, p3_recv, in_sem,
+    mpartial, bpartial, topics_z, q3, p2_send, p2_recv, p3_recv, in_sem, here_sem, line_sem,
     w_send, w_recv, t_send, t_recv, x_send, x_recv, a_send, a_recv, r_send, r_recv,
     z_send, z_recv, g_send, g_recv, b_send, b_recv, u_send, u_recv, e_send, e_recv, s_send, s_recv, m_send, m_recv,
     *, np_, nz,
@@ -97,7 +97,7 @@
     b = lax.axis_index("doc")
     xh, z, c = b // (nz * NC), (b // NC) % nz, b % NC
     w = xh * NC + c
-    chunk = k // 4
+    chunk, chunk2 = k // 4, k // 2
     slab = wb // np_
 
     def w_device(at):
@@ -131,15 +131,28 @@
         load.start()
 
     barrier = pltpu.get_barrier_semaphore()
-    for peer in w_peers:
-        pl.semaphore_signal(barrier, inc=1, device_id=w_device(peer), device_id_type=MESH)
-    for peer in z_peers:
-        pl.semaphore_signal(barrier, inc=1, device_id=z_device(peer), device_id_type=MESH)
-    for peer in p_peers:
-        pl.semaphore_signal(barrier, inc=1, device_id=p_device(peer), device_id_type=MESH)
+    ny = np_ // NX
+    xl, y = p // ny, p % ny
+    y_next = [p_device(xl * ny + lax.rem(y + step, ny)) for step in (1, ny - 1)]
+    x_across = p_device((NX - 1 - xl) * ny + y)
+    near = [w_device(peer) for peer in w_peers] + [z_device(z_peers[0]), z_device(z_peers[-1])] + y_next + [x_across]
+    for device in near:
+        pl.semaphore_signal(barrier, inc=1, device_id=device, device_id_type=MESH)
 
     loads[0].wait()
-    pl.semaphore_wait(barrier, NW - 1 + nz - 1 + np_ - 1)
+    pl.semaphore_wait(barrier, len(near))
+
+    def tell(stage):
+        if stage > 0:
+            for way in (0, 1):
+                pl.semaphore_wait(here_sem.at[way, stage - 1], 1)
+        if stage < ny // 2 - 1:
+            for way in (0, 1):
+                pl.semaphore_signal(here_sem.at[way, stage], inc=1, device_id=y_next[way], device_id_type=MESH)
+        else:
+            pl.semaphore_signal(line_sem.at[0], inc=1, device_id=x_across, device_id_type=MESH)
+
+    tell(0)
 
     sends = []
 
@@ -178,10 +191,10 @@
                 remote(
                     here, here, r_send.at[way, far - 1, ch], r_recv.at[way, far - 1, ch], z_device(ring_block(1 - way, 1))
                 ).wait_recv()
-                if far == last - 2 and ch // 2 == way:
-                    start(ring_copy(way, far, ch, 2))
                 if far < last - 1:
                     start(ring_copy(way, far, ch, 1))
+            if far == last - 2:
+                start(ring_copy(ch // 2, far, ch, 2))
 
     def blocks_at(far):
         if far == 0 or far == last:
@@ -293,13 +306,16 @@
         for i, peer in enumerate(z_peers):
             start(remote(data4.at[:, peer], data32.at[z], z_send.at[i], z_recv.at[z], z_device(peer)))
         data32[z] = data4[:, z]
+        tell(1)
 
     product, col_total = exchange(mpartial, 0, w, w_peers, w_device, (a_send, a_recv), acc, columns, own_words)
     topics = topics * product / col_total
     for update in range(1, UPDATES):
         stacked = stack_topics(topics)
         acc = sum(block_term(stacked, rows_of(at), dsplit, at) for at in range(nz))
-        product, _ = exchange(mpartial, update, w, w_peers, w_device, (a_send, a_recv), acc, None)
+        product, _ = exchange(
+            mpartial, update, w, w_peers, w_device, (a_send, a_recv), acc, None, functools.partial(tell, update + 1)
+        )
         topics = topics * product / col_total
 
     topics_z[z] = pack(topics)
@@ -331,6 +347,7 @@
     aligned = dot(
         jnp.concatenate(split3(turn_flat(new_dict)), axis=1), jnp.concatenate([onehot, onehot, onehot], axis=0)
     )
+    pl.semaphore_wait(line_sem.at[0], 1)
     for at in range(np_):
         p2_send[at] = pack(aligned[at * slab : (at + 1) * slab])
     for i, peer in enumerate(p_peers):
@@ -354,16 +371,33 @@
         remote(p3_recv.at[p], p3_recv.at[peer], m_send.at[i], m_recv.at[peer], p_device(peer)).wait_recv()
 
     mgather[w] = turn_tall(jnp.concatenate([unpack(p3_recv[at]) for at in range(np_)], axis=0))
-    for i, peer in enumerate(w_peers):
-        start(remote(mgather.at[w], mgather.at[w], x_send.at[i], x_recv.at[w], w_device(peer)))
-    split_block(mgather, msplit, w)
-    columns = column_term(msplit, w)
-    acc = block_term(stacked, bdata[w], msplit, w)
-    for i, peer in enumerate(w_peers):
-        remote(mgather.at[w], mgather.at[peer], x_send.at[i], x_recv.at[peer], w_device(peer)).wait_recv()
-        split_block(mgather, msplit, peer)
-        columns = columns + column_term(msplit, peer)
-        acc = acc + block_term(stacked, bdata[peer], msplit, peer)
+    partner, across = xh * NC + (NC - 1 - c), lax.rem(w + NC, NW)
+
+    def median_copy(number, block, part, to):
+        at = mgather.at[block, pl.ds(part * chunk2, chunk2), :]
+        return remote(at, at, x_send.at[number, part], x_recv.at[block, part], w_device(to))
+
+    for part in (0, 1):
+        start(median_copy(0, w, part, across))
+    for part in (0, 1):
+        start(median_copy(1, w, part, partner))
+
+    def add_block(at, columns, acc):
+        split_block(mgather, msplit, at)
+        return columns + column_term(msplit, at), acc + block_term(stacked, bdata[at], msplit, at)
+
+    columns, acc = add_block(w, jnp.zeros((8, 2 * k), F32), jnp.zeros((topics.shape[0], 2 * k), F32))
+    for part in (0, 1):
+        median_copy(0, across, part, across).wait_recv()
+        start(median_copy(2, across, part, partner))
+    for part in (0, 1):
+        median_copy(1, partner, part, partner).wait_recv()
+    columns, acc = add_block(partner, columns, acc)
+    columns, acc = add_block(across, columns, acc)
+    far_block = lax.rem(partner + NC, NW)
+    for part in (0, 1):
+        median_copy(2, far_block, part, partner).wait_recv()
+    columns, acc = add_block(far_block, columns, acc)
     product, col_total = exchange(bpartial, 0, z, z_peers, z_device, (e_send, e_recv), acc, columns)
     topics = topics * product / col_total
     for update in range(1, REFITS):
@@ -412,9 +446,12 @@
         pltpu.VMEM((np_, slab // 2, 2 * k), F32),
         pltpu.VMEM((np_, slab // 2, 2 * k), F32),
         sem((7,)),
+        pltpu.SemaphoreType.REGULAR((2, np_ // NX // 2 - 1)),
+        pltpu.SemaphoreType.REGULAR((1,)),
     ]
-    for _ in range(3):
+    for _ in range(2):
         scratch += [sem((NW - 1,)), sem((NW,))]
+    scratch += [sem((3, 2)), sem((NW, 2))]
     scratch += [sem((UPDATES, NW - 1)), sem((UPDATES, NW))]
     scratch += [sem((2, last, 4)), sem((2, last, 4))]
     for _ in range(4):

time: 84.7 us -> 83 us (0.980)
  Pallas kernels: 81.9 us -> 80.2 us
    pallas_call x1, Pallas kernels: 81.9 us -> 80.2 us  [per_device(): pl.pallas_call(functools.partial(kernel, np_=np_, nz=nz), out_shape=(jax....]
where the time goes in v4:
time: 83 us; the launch traced here: 82.8 us
  Pallas kernels  80.2 us (97%)
  local copies, waits for them, and re-layouts  1.91 us (2%)
    pallas_call x1, Pallas kernels, per_device(): pl.pallas_call(functools.partial(kernel, np_=np_, nz=nz), out_shape=(jax....  80.2 us
    unnamed x4, local copies, waits for them, and re-layouts  1.91 us

profile of v4, /device:TPU:1, one launch (start us, length us, event | category | flops | bytes accessed | tf_op | source)
XLA Modules:
  0.0 82.8 jit_solution(5064923285123236050)
XLA Ops:
  0.6 80.2 %shard_map.86 = (f32[32,64]{1,0:T(8,128)}, f32[4,64]{1,0:T(4,128)}) custom-call(s32[8,16384]{1,0:T(8,128)} %bitcast.7, s32[8,128]{1,0:T(8,128)} %bitcast.10, f32[8,64]{1,0:T(8,128)} %bitcast.11, f32[64,512]{1,0:T(8,128)} %bitcast.8, s32[1,64]{1,0:T(1,128)} %perm_ref.1, s32[4,16384]{1,0:T(4,128)} %base_ref.1, f32[4,64]{1,0:T(4,128)} %btop_ref.1), custom_call_target="tpu_custom_call" | custom-call | tf_op jit(solution)/shard_map/pallas_call | solution.py:464
  80.9 0.0 copy-start
  80.9 1.3 %copy.11 = f32[1,1,32,64]{3,2,1,0:T(8,128)} copy(f32[1,1,32,64]{3,2,1,0:T(8,128)} %bitcast.9) | data formatting | bytes 16384
  82.2 0.0 copy-done
  82.2 0.6 copy.12
Async XLA Ops:
  80.9 1.3 %copy-start = (f32[4,64]{1,0:T(4,128)S(1)}, f32[4,64]{1,0:T(4,128)}, u32[]{:S(2)}) copy-start(f32[4,64]{1,0:T(4,128)} %get-tuple-element.9) | copy-start | bytes 3076

commit v5 on v4

--- a/solution.py
+++ b/solution.py
@@ -86,7 +86,7 @@
     med_ref, refit_ref,
     counts_in, mask_in, perm_in, base_in,
     masked, data4, data32, bsend, base8, bdata, mtop4, btop8, dgather, mgather, dsplit, msplit,
-    mpartial, bpartial, topics_z, q3, p2_send, p2_recv, p3_recv, in_sem, here_sem, line_sem,
+    mpartial, bpartial, topics_z, q3, p2_send, p2_recv, p3_recv, in_sem, here_sem, line_sem, fsend, frecv, f_send, f_recv,
     w_send, w_recv, t_send, t_recv, x_send, x_recv, a_send, a_recv, r_send, r_recv,
     z_send, z_recv, g_send, g_recv, b_send, b_recv, u_send, u_recv, e_send, e_recv, s_send, s_recv, m_send, m_recv,
     *, np_, nz,
@@ -321,23 +321,23 @@
     topics_z[z] = pack(topics)
     for i, peer in enumerate(z_peers):
         start(remote(topics_z.at[z], topics_z.at[z], g_send.at[i], g_recv.at[z], z_device(peer)))
-    for i, peer in enumerate(z_peers):
-        remote(topics_z.at[z], topics_z.at[peer], g_send.at[i], g_recv.at[peer], z_device(peer)).wait_recv()
-    for i, peer in enumerate(z_peers):
-        remote(data4.at[:, peer], data32.at[peer], z_send.at[i], z_recv.at[peer], z_device(peer)).wait_recv()
-    for i, peer in enumerate(z_peers):
-        start(remote(bsend.at[:, peer], base8.at[z], b_send.at[i], b_recv.at[z], z_device(peer)))
-        start(remote(btop8.at[z], btop8.at[z], u_send.at[i], u_recv.at[z], z_device(peer)))
-    base8[z] = bsend[:, z]
     rows = NW * docs
-    every = jnp.concatenate([unpack(topics_z[at]) for at in range(nz)], axis=0)
-
-    for at in range(nz):
-        recon = dot(stack_topics(every[at * rows : (at + 1) * rows]), dsplit[z])
+
+    def add_quotient(at):
+        recon = dot(stack_topics(unpack(topics_z[at])), dsplit[z])
         data = jnp.concatenate([data32[at, owner] for owner in range(NW)], axis=0)
         high, low = split2(data / recon)
         for part, piece in enumerate((high, low, high)):
-            q3[(part * nz + at) * rows : (part * nz + at + 1) * rows] = piece
+            q3[pl.ds(pl.multiple_of((part * nz + at) * rows, rows), rows)] = piece
+
+    add_quotient(z)
+    order = [i for far in range(nz // 2) for i in sorted({far, nz - 2 - far})]
+    for i in order:
+        peer = z_peers[i]
+        remote(data4.at[:, peer], data32.at[peer], z_send.at[i], z_recv.at[peer], z_device(peer)).wait_recv()
+        remote(topics_z.at[z], topics_z.at[peer], g_send.at[i], g_recv.at[peer], z_device(peer)).wait_recv()
+        add_quotient(peer)
+    every = jnp.concatenate([unpack(topics_z[at]) for at in range(nz)], axis=0)
     wide = turn_tall(every)
     high, low = split2(wide)
     numerator = dot(jnp.concatenate([high, high, low], axis=1), q3[...])
@@ -353,6 +353,10 @@
     for i, peer in enumerate(p_peers):
         start(remote(p2_send.at[peer], p2_recv.at[p], s_send.at[i], s_recv.at[p], p_device(peer)))
     p2_recv[p] = p2_send[p]
+    for i, peer in enumerate(z_peers):
+        start(remote(bsend.at[:, peer], base8.at[z], b_send.at[i], b_recv.at[z], z_device(peer)))
+        start(remote(btop8.at[z], btop8.at[z], u_send.at[i], u_recv.at[z], z_device(peer)))
+    base8[z] = bsend[:, z]
     for i, peer in enumerate(p_peers):
         remote(p2_send.at[peer], p2_recv.at[peer], s_send.at[i], s_recv.at[peer], p_device(peer)).wait_recv()
     median = middle([p2_recv[at] for at in range(np_)])
@@ -360,6 +364,20 @@
     for i, peer in enumerate(p_peers):
         start(remote(p3_recv.at[p], p3_recv.at[p], m_send.at[i], m_recv.at[p], p_device(peer)))
     med_ref[...] = unpack(median)
+    for i, peer in enumerate(p_peers):
+        remote(p3_recv.at[p], p3_recv.at[peer], m_send.at[i], m_recv.at[peer], p_device(peer)).wait_recv()
+
+    mgather[w] = turn_tall(jnp.concatenate([unpack(p3_recv[at]) for at in range(np_)], axis=0))
+    partner, across = xh * NC + (NC - 1 - c), lax.rem(w + NC, NW)
+
+    def median_copy(number, block, part, to):
+        at = mgather.at[block, pl.ds(part * chunk2, chunk2), :]
+        return remote(at, at, x_send.at[number, part], x_recv.at[block, part], w_device(to))
+
+    for part in (0, 1):
+        start(median_copy(0, w, part, across))
+    for part in (0, 1):
+        start(median_copy(1, w, part, partner))
     for i, peer in enumerate(z_peers):
         remote(bsend.at[:, peer], base8.at[peer], b_send.at[i], b_recv.at[peer], z_device(peer)).wait_recv()
         remote(btop8.at[z], btop8.at[peer], u_send.at[i], u_recv.at[peer], z_device(peer)).wait_recv()
@@ -367,20 +385,6 @@
         bdata[owner] = jnp.concatenate([base8[at, owner] for at in range(nz)], axis=0)
     topics = jnp.concatenate([btop8[at] for at in range(nz)], axis=0)
     stacked = stack_topics(topics)
-    for i, peer in enumerate(p_peers):
-        remote(p3_recv.at[p], p3_recv.at[peer], m_send.at[i], m_recv.at[peer], p_device(peer)).wait_recv()
-
-    mgather[w] = turn_tall(jnp.concatenate([unpack(p3_recv[at]) for at in range(np_)], axis=0))
-    partner, across = xh * NC + (NC - 1 - c), lax.rem(w + NC, NW)
-
-    def median_copy(number, block, part, to):
-        at = mgather.at[block, pl.ds(part * chunk2, chunk2), :]
-        return remote(at, at, x_send.at[number, part], x_recv.at[block, part], w_device(to))
-
-    for part in (0, 1):
-        start(median_copy(0, w, part, across))
-    for part in (0, 1):
-        start(median_copy(1, w, part, partner))
 
     def add_block(at, columns, acc):
         split_block(mgather, msplit, at)
@@ -388,11 +392,11 @@
 
     columns, acc = add_block(w, jnp.zeros((8, 2 * k), F32), jnp.zeros((topics.shape[0], 2 * k), F32))
     for part in (0, 1):
+        median_copy(1, partner, part, partner).wait_recv()
+    columns, acc = add_block(partner, columns, acc)
+    for part in (0, 1):
         median_copy(0, across, part, across).wait_recv()
         start(median_copy(2, across, part, partner))
-    for part in (0, 1):
-        median_copy(1, partner, part, partner).wait_recv()
-    columns, acc = add_block(partner, columns, acc)
     columns, acc = add_block(across, columns, acc)
     far_block = lax.rem(partner + NC, NW)
     for part in (0, 1):
@@ -400,15 +404,27 @@
     columns, acc = add_block(far_block, columns, acc)
     product, col_total = exchange(bpartial, 0, z, z_peers, z_device, (e_send, e_recv), acc, columns)
     topics = topics * product / col_total
-    for update in range(1, REFITS):
+    for update in range(1, REFITS - 1):
         stacked = stack_topics(topics)
         acc = sum(block_term(stacked, bdata[at], msplit, at) for at in range(NW))
         product, _ = exchange(bpartial, update, z, z_peers, z_device, (e_send, e_recv), acc, None)
         topics = topics * product / col_total
+    stacked = stack_topics(topics)
+    part = fold(sum(block_term(stacked, bdata[at], msplit, at) for at in range(NW)))
+    for at in range(nz):
+        fsend[at] = part[at * bdocs : (at + 1) * bdocs]
+    for i, peer in enumerate(z_peers):
+        start(remote(fsend.at[peer], frecv.at[z], f_send.at[i], f_recv.at[z], z_device(peer)))
+    frecv[z] = fsend[z]
     own = topics[0:bdocs]
     for at in range(1, nz):
         own = jnp.where(z == at, topics[at * bdocs : (at + 1) * bdocs], own)
-    refit_ref[...] = own
+    for i, peer in enumerate(z_peers):
+        remote(fsend.at[peer], frecv.at[peer], f_send.at[i], f_recv.at[peer], z_device(peer)).wait_recv()
+    product = frecv[0]
+    for at in range(1, nz):
+        product = product + frecv[at]
+    refit_ref[...] = own * product / col_total
 
     for copy in sends:
         copy.wait_send()
@@ -448,6 +464,10 @@
         sem((7,)),
         pltpu.SemaphoreType.REGULAR((2, np_ // NX // 2 - 1)),
         pltpu.SemaphoreType.REGULAR((1,)),
+        pltpu.VMEM((nz, bdocs, k), F32),
+        pltpu.VMEM((nz, bdocs, k), F32),
+        sem((nz - 1,)),
+        sem((nz,)),
     ]
     for _ in range(2):
         scratch += [sem((NW - 1,)), sem((NW,))]

time: 83 us -> 81.6 us (0.983)
  Pallas kernels: 80.2 us -> 78.8 us
    pallas_call x1, Pallas kernels: 80.2 us -> 78.8 us  [per_device(): pl.pallas_call(functools.partial(kernel, np_=np_, nz=nz), out_shape=(jax....]
where the time goes in v5:
time: 81.6 us; the launch traced here: 81.4 us
  Pallas kernels  78.8 us (97%)
  local copies, waits for them, and re-layouts  1.91 us (2%)
    pallas_call x1, Pallas kernels, per_device(): pl.pallas_call(functools.partial(kernel, np_=np_, nz=nz), out_shape=(jax....  78.8 us
    unnamed x4, local copies, waits for them, and re-layouts  1.91 us

profile of v5, /device:TPU:1, one launch (start us, length us, event | category | flops | bytes accessed | tf_op | source)
XLA Modules:
  0.0 81.4 jit_solution(13894855925200976719)
XLA Ops:
  0.6 78.8 %shard_map.86 = (f32[32,64]{1,0:T(8,128)}, f32[4,64]{1,0:T(4,128)}) custom-call(s32[8,16384]{1,0:T(8,128)} %bitcast.7, s32[8,128]{1,0:T(8,128)} %bitcast.10, f32[8,64]{1,0:T(8,128)} %bitcast.11, f32[64,512]{1,0:T(8,128)} %bitcast.8, s32[1,64]{1,0:T(1,128)} %perm_ref.1, s32[4,16384]{1,0:T(4,128)} %base_ref.1, f32[4,64]{1,0:T(4,128)} %btop_ref.1), custom_call_target="tpu_custom_call" | custom-call | tf_op jit(solution)/shard_map/pallas_call | solution.py:484
  79.5 0.0 copy-start
  79.5 1.3 %copy.11 = f32[1,1,32,64]{3,2,1,0:T(8,128)} copy(f32[1,1,32,64]{3,2,1,0:T(8,128)} %bitcast.9) | data formatting | bytes 16384
  80.8 0.0 copy-done
  80.8 0.6 copy.12
Async XLA Ops:
  79.5 1.3 %copy-start = (f32[4,64]{1,0:T(4,128)S(1)}, f32[4,64]{1,0:T(4,128)}, u32[]{:S(2)}) copy-start(f32[4,64]{1,0:T(4,128)} %get-tuple-element.9) | copy-start | bytes 3076

commit v6 on v5

--- a/solution.py
+++ b/solution.py
@@ -111,7 +111,9 @@
 
     w_peers = [lax.rem(w + i, NW) for i in range(1, NW)]
     z_peers = [lax.rem(z + i, nz) for i in range(1, nz)]
-    p_peers = [lax.rem(p + i, np_) for i in range(1, np_)]
+    p_steps = sorted(range(1, np_), key=lambda i: -min(i % (np_ // NX), -i % (np_ // NX)))
+    p_peers = [lax.rem(p + i, np_) for i in p_steps]
+    z_far = sorted(enumerate(z_peers), key=lambda pair: abs(pair[0] + 1 - nz // 2))
 
     loads = [
         pltpu.make_async_copy(src, dst, in_sem.at[i])
@@ -319,7 +321,7 @@
         topics = topics * product / col_total
 
     topics_z[z] = pack(topics)
-    for i, peer in enumerate(z_peers):
+    for i, peer in z_far:
         start(remote(topics_z.at[z], topics_z.at[z], g_send.at[i], g_recv.at[z], z_device(peer)))
     rows = NW * docs
 
@@ -413,7 +415,7 @@
     part = fold(sum(block_term(stacked, bdata[at], msplit, at) for at in range(NW)))
     for at in range(nz):
         fsend[at] = part[at * bdocs : (at + 1) * bdocs]
-    for i, peer in enumerate(z_peers):
+    for i, peer in z_far:
         start(remote(fsend.at[peer], frecv.at[z], f_send.at[i], f_recv.at[z], z_device(peer)))
     frecv[z] = fsend[z]
     own = topics[0:bdocs]

time: 81.6 us -> 80.7 us (0.989)
    pallas_call x1, Pallas kernels: 78.8 us -> 78 us  [per_device(): pl.pallas_call(functools.partial(kernel, np_=np_, nz=nz), out_shape=(jax....]
where the time goes in v6:
time: 80.7 us; the launch traced here: 80.5 us
  Pallas kernels  78 us (97%)
  local copies, waits for them, and re-layouts  1.91 us (2%)
    pallas_call x1, Pallas kernels, per_device(): pl.pallas_call(functools.partial(kernel, np_=np_, nz=nz), out_shape=(jax....  78 us
    unnamed x4, local copies, waits for them, and re-layouts  1.91 us

profile of v6, /device:TPU:1, one launch (start us, length us, event | category | flops | bytes accessed | tf_op | source)
XLA Modules:
  0.0 80.5 jit_solution(13210807802995267315)
XLA Ops:
  0.6 78.0 %shard_map.86 = (f32[32,64]{1,0:T(8,128)}, f32[4,64]{1,0:T(4,128)}) custom-call(s32[8,16384]{1,0:T(8,128)} %bitcast.7, s32[8,128]{1,0:T(8,128)} %bitcast.10, f32[8,64]{1,0:T(8,128)} %bitcast.11, f32[64,512]{1,0:T(8,128)} %bitcast.8, s32[1,64]{1,0:T(1,128)} %perm_ref.1, s32[4,16384]{1,0:T(4,128)} %base_ref.1, f32[4,64]{1,0:T(4,128)} %btop_ref.1), custom_call_target="tpu_custom_call" | custom-call | tf_op jit(solution)/shard_map/pallas_call | solution.py:486
  78.6 0.0 copy-start
  78.6 1.3 %copy.11 = f32[1,1,32,64]{3,2,1,0:T(8,128)} copy(f32[1,1,32,64]{3,2,1,0:T(8,128)} %bitcast.9) | data formatting | bytes 16384
  79.9 0.0 copy-done
  79.9 0.6 copy.12
Async XLA Ops:
  78.6 1.3 %copy-start = (f32[4,64]{1,0:T(4,128)S(1)}, f32[4,64]{1,0:T(4,128)}, u32[]{:S(2)}) copy-start(f32[4,64]{1,0:T(4,128)} %get-tuple-element.9) | copy-start | bytes 3076
